TPU v7x, 32 devices: a whole 2x2x4 slice. The times are simulated.
32 devices in a mesh: section: 4 (over y, core), tok: 8 (over z, x).
Axes of the slice: x: 2, y: 2, z: 4, core: 2. Of those that a mesh axis runs over, the one named last changes fastest.
Arguments:
- patches: bfloat16 [1024, 6144], P('tok'), may hold values from -6 to 6
- patch_ids: int32 [1024], P('tok'), may hold values from 0 to 255
- pos_table: bfloat16 [256, 6144], replicated, may hold values from -5 to 5
- token_counts: int32 [8], P('tok'), may hold values from 16 to 128, as said below
- norm_gain: float32 [4, 6144], P('section'), may hold values from 0.25 to 1.75
- norm_bias: float32 [4, 6144], P('section'), may hold values from -3 to 3
- branch_scale: float32 [4, 6144], P('section'), may hold values from 0.5 to 2
- act_range: float32 [4, 6144], P('section'), may hold values from 1 to 8
- weight_range: float32 [4, 6144], P('section'), may hold values from 0.125 to 1
- alpha_index: int32 [4], P('section'), may hold values from 2 to 7
Outputs:
- covariance: float32 [4, 128, 6144], P('section')
- channel_mean: float32 [4, 6144], P('section')
Inputs may be any that keep to these rules, and one draw needn't show every extreme that they name: Each shard's calibration tokens are its first token_counts slots; at least one shard is full in every draw.
All inputs are finite; a program needn't handle non-finite values.
Results may differ from a plain program's by a relative error of at most 0.0067.
Values may be sent and summed in bfloat16 or wider, within the bound.
No kernel may reach another device: no remote copies, remote signals or barrier semaphores. Data moves between devices by JAX's collectives and lax.ppermute only.
A program may use at most 256 MiB of HBM per device.

v0:
```python
import jax
import jax.numpy as jnp
from jax import lax
from jax.sharding import PartitionSpec as P

BLOCK = 128
MICRO = 4


def from_behind(block, axis, distance):
    devices = range(lax.axis_size(axis))
    route = [(i - distance, i) for i in devices if i - distance in devices]
    return lax.ppermute(block, axis, route)


def layer_norm(values, gain, bias_row):
    centre = jnp.mean(values, axis=-1, keepdims=True)
    spread = jnp.mean(jnp.square(values - centre), axis=-1, keepdims=True)
    return (values - centre) * lax.rsqrt(spread + 1e-06) * gain + bias_row


def smoothing(act_row, weight_row, alpha_code):
    exponent = alpha_code.astype(jnp.float32) / 8.0
    return jnp.exp(exponent * jnp.log(act_row) + (exponent - 1.0) * jnp.log(weight_row))


def about_mean(sum_second, sum_first, own_count, mean_row):
    cross = (
        sum_first[:BLOCK][:, None] * mean_row[None, :]
        + mean_row[:BLOCK][:, None] * sum_first[None, :]
    )
    return sum_second - cross + own_count * (mean_row[:BLOCK][:, None] * mean_row[None, :])


def body(
    patches,
    patch_ids,
    pos_table,
    token_counts,
    norm_gain,
    norm_bias,
    branch_scale,
    act_range,
    weight_range,
    alpha_index,
):
    sections = lax.axis_size("section")
    section_index = lax.axis_index("section")
    rows_here = patches.shape[0]
    width = patches.shape[1]
    micro_rows = rows_here // MICRO
    looked_up = jnp.take(pos_table, patch_ids, axis=0).astype(jnp.float32)
    start_rows = (patches.astype(jnp.float32) + looked_up).astype(jnp.bfloat16)
    positions = jnp.arange(rows_here, dtype=jnp.int32)
    valid_flat = (positions < token_counts[0]).astype(jnp.float32)
    factor = smoothing(act_range[0], weight_range[0], alpha_index[0])
    blocks = start_rows.reshape(MICRO, micro_rows, width)
    valid_rows = valid_flat.reshape(MICRO, micro_rows)

    def tick_step(tick, carry):
        incoming, stash = carry
        micro_index = tick - section_index
        active = jnp.logical_and(micro_index >= 0, micro_index < MICRO)
        safe_index = jnp.clip(micro_index, 0, MICRO - 1)
        own_block = lax.dynamic_index_in_dim(blocks, safe_index, 0, keepdims=False)
        current = jnp.where(section_index == 0, own_block, incoming)
        normed = layer_norm(current.astype(jnp.float32), norm_gain[0], norm_bias[0])
        smoothed = (normed / factor).astype(jnp.bfloat16)
        weight_mask = lax.dynamic_index_in_dim(valid_rows, safe_index, 0, keepdims=False).astype(
            jnp.bfloat16
        )
        masked = smoothed * weight_mask[:, None]
        previous = lax.dynamic_index_in_dim(stash, safe_index, 0, keepdims=False)
        kept = jnp.where(active, masked, previous)
        stash = lax.dynamic_update_index_in_dim(stash, kept, safe_index, 0)
        updated = (current.astype(jnp.float32) + branch_scale[0] * jax.nn.gelu(normed)).astype(
            jnp.bfloat16
        )
        passed = from_behind(updated, "section", 1)
        return (passed, stash)

    initial = (
        jnp.zeros((micro_rows, width), jnp.bfloat16),
        jnp.zeros((MICRO, micro_rows, width), jnp.bfloat16),
    )
    carried = lax.fori_loop(0, sections + MICRO - 1, tick_step, initial)
    masked = carried[1].reshape(rows_here, width)
    ones_row = jnp.ones((1, rows_here), jnp.bfloat16)
    sum_first = jnp.dot(ones_row, masked, preferred_element_type=jnp.float32)[0]
    sum_second = lax.dot_general(
        masked[:, :BLOCK], masked, (((0,), (0,)), ((), ())), preferred_element_type=jnp.float32
    )
    own_count = token_counts.astype(jnp.float32)
    total_count, channel_sums = lax.psum((own_count, sum_first), "tok")
    mean_row = channel_sums / total_count
    gram_block = lax.psum(about_mean(sum_second, sum_first, own_count, mean_row), "tok")
    return ((gram_block / total_count)[None], mean_row[None])


def solution(mesh):
    in_specs = (
        P("tok", None),
        P("tok"),
        P(),
        P("tok"),
        P("section", None),
        P("section", None),
        P("section", None),
        P("section", None),
        P("section", None),
        P("section"),
    )
    out_specs = (P("section", None, None), P("section", None))
    return jax.shard_map(body, mesh=mesh, in_specs=in_specs, out_specs=out_specs, check_vma=False)
```

profile of v0, /device:TPU:0, one launch (start us, length us, event | category | flops | bytes accessed | tf_op | source)
XLA Modules:
  0.0 289.3 jit_solution(6521652200142624331)
XLA Ops:
  7.2 0.8 compare_and_fusion
  8.0 0.7 compare_select_fusion
  10.2 2.6 gather_fusion
  12.8 0.7 add_exponential_fusion
  13.5 3.6 %add_convert_fusion = bf16[128,6144]{1,0:T(8,128)(2,1)} fusion(bf16[128,6144]{1,0:T(8,128)(2,1)} %param.12, bf16[128,6144]{1,0:T(8,128)(2,1)} %gather_fusion, pred[128]{0:T(512)(128)(4,1)S(1)} %compare_and_fusion), kind=kLoop, calls=%fused_computation.34 | loop fusion | flops 3932160 | bytes 4718720 | tf_op jit(solution)/shard_map/convert_element_type | solution.py:53
  17.1 0.8 broadcast_in_dim.53
  17.9 1.3 broadcast_in_dim.54
  19.2 84.4 %while.16 = (s32[]{:T(128)}, bf16[32,6144]{1,0:T(8,128)(2,1)}, bf16[4,32,6144]{2,1,0:T(8,128)(2,1)}, pred[]{:T(512)}, s32[]{:T(128)}, /*index=5*/bf16[4,32,6144]...) while((s32[]{:T(128)}, bf16[32,6144]{1,0:T(8,128)(2,1)}, ...), condition=%wide.region_3.4_spmd, body=%wide.region_0.3_spmd.sunk | while | flops 6881320 | bytes 6342548 | solution.py:86
  19.2 1.3 convert_reduce_fusion.2
  20.8 1.3 fusion.32
  22.1 3.3 %collective-permute-start = (bf16[32,6144]{1,0:T(8,128)(2,1)}, bf16[32,6144]{1,0:T(8,128)(2,1)}, u32[]{:S(2)}, u32[]{:S(2)}) collective-permute-start(bf16[32,6144]{1,0:T(8,128)(2,1)} %fusion.32), channel_id=1, source_target_pairs={{0,8},{8,16},{16,24},{1,9},{9,17},{17,25},{2,10},{10,18},{18,26},{... | collective-permute-start | bytes 1179656 | tf_op jit(solution)/shard_map/while/body/eval_jaxpr/ppermute | solution.py:13
  25.4 1.8 constant_dynamic-slice_fusion.3
  27.1 2.1 bitcast_dynamic-update-slice_fusion.2
  29.2 1.2 convert_reduce_fusion.2
  30.8 1.3 fusion.32
  32.1 5.8 %collective-permute-start = (bf16[32,6144]{1,0:T(8,128)(2,1)}, bf16[32,6144]{1,0:T(8,128)(2,1)}, u32[]{:S(2)}, u32[]{:S(2)}) collective-permute-start(bf16[32,6144]{1,0:T(8,128)(2,1)} %fusion.32), channel_id=1, source_target_pairs={{0,8},{8,16},{16,24},{1,9},{9,17},{17,25},{2,10},{10,18},{18,26},{... | collective-permute-start | bytes 1179656 | tf_op jit(solution)/shard_map/while/body/eval_jaxpr/ppermute | solution.py:13
  37.9 1.8 constant_dynamic-slice_fusion.3
  39.7 2.1 bitcast_dynamic-update-slice_fusion.2
  41.8 1.2 convert_reduce_fusion.2
  43.3 1.3 fusion.32
  44.6 5.6 %collective-permute-start = (bf16[32,6144]{1,0:T(8,128)(2,1)}, bf16[32,6144]{1,0:T(8,128)(2,1)}, u32[]{:S(2)}, u32[]{:S(2)}) collective-permute-start(bf16[32,6144]{1,0:T(8,128)(2,1)} %fusion.32), channel_id=1, source_target_pairs={{0,8},{8,16},{16,24},{1,9},{9,17},{17,25},{2,10},{10,18},{18,26},{... | collective-permute-start | bytes 1179656 | tf_op jit(solution)/shard_map/while/body/eval_jaxpr/ppermute | solution.py:13
  50.3 1.8 constant_dynamic-slice_fusion.3
  52.0 2.1 bitcast_dynamic-update-slice_fusion.2
  54.1 1.2 convert_reduce_fusion.2
  55.7 1.3 fusion.32
  57.0 5.7 %collective-permute-start = (bf16[32,6144]{1,0:T(8,128)(2,1)}, bf16[32,6144]{1,0:T(8,128)(2,1)}, u32[]{:S(2)}, u32[]{:S(2)}) collective-permute-start(bf16[32,6144]{1,0:T(8,128)(2,1)} %fusion.32), channel_id=1, source_target_pairs={{0,8},{8,16},{16,24},{1,9},{9,17},{17,25},{2,10},{10,18},{18,26},{... | collective-permute-start | bytes 1179656 | tf_op jit(solution)/shard_map/while/body/eval_jaxpr/ppermute | solution.py:13
  62.6 1.8 constant_dynamic-slice_fusion.3
  64.4 2.1 bitcast_dynamic-update-slice_fusion.2
  66.5 1.2 convert_reduce_fusion.2
  68.1 1.3 fusion.32
  69.4 5.6 %collective-permute-start = (bf16[32,6144]{1,0:T(8,128)(2,1)}, bf16[32,6144]{1,0:T(8,128)(2,1)}, u32[]{:S(2)}, u32[]{:S(2)}) collective-permute-start(bf16[32,6144]{1,0:T(8,128)(2,1)} %fusion.32), channel_id=1, source_target_pairs={{0,8},{8,16},{16,24},{1,9},{9,17},{17,25},{2,10},{10,18},{18,26},{... | collective-permute-start | bytes 1179656 | tf_op jit(solution)/shard_map/while/body/eval_jaxpr/ppermute | solution.py:13
  75.0 1.8 constant_dynamic-slice_fusion.3
  76.8 2.1 bitcast_dynamic-update-slice_fusion.2
  78.9 1.2 convert_reduce_fusion.2
  80.5 1.3 fusion.32
  81.7 5.6 %collective-permute-start = (bf16[32,6144]{1,0:T(8,128)(2,1)}, bf16[32,6144]{1,0:T(8,128)(2,1)}, u32[]{:S(2)}, u32[]{:S(2)}) collective-permute-start(bf16[32,6144]{1,0:T(8,128)(2,1)} %fusion.32), channel_id=1, source_target_pairs={{0,8},{8,16},{16,24},{1,9},{9,17},{17,25},{2,10},{10,18},{18,26},{... | collective-permute-start | bytes 1179656 | tf_op jit(solution)/shard_map/while/body/eval_jaxpr/ppermute | solution.py:13
  87.4 1.8 constant_dynamic-slice_fusion.3
  89.2 2.1 bitcast_dynamic-update-slice_fusion.2
  91.3 1.2 convert_reduce_fusion.2
  92.9 1.3 fusion.32
  94.1 5.6 %collective-permute-start = (bf16[32,6144]{1,0:T(8,128)(2,1)}, bf16[32,6144]{1,0:T(8,128)(2,1)}, u32[]{:S(2)}, u32[]{:S(2)}) collective-permute-start(bf16[32,6144]{1,0:T(8,128)(2,1)} %fusion.32), channel_id=1, source_target_pairs={{0,8},{8,16},{16,24},{1,9},{9,17},{17,25},{2,10},{10,18},{18,26},{... | collective-permute-start | bytes 1179656 | tf_op jit(solution)/shard_map/while/body/eval_jaxpr/ppermute | solution.py:13
  99.8 1.8 constant_dynamic-slice_fusion.3
  101.5 2.1 bitcast_dynamic-update-slice_fusion.2
  103.6 1.7 fusion.23
  105.3 37.9 %all-reduce = (f32[6144]{0:T(1024)S(1)}, f32[]{:T(128)}) all-reduce(f32[6144]{0:T(1024)S(1)} %bitcast.49, f32[]{:T(128)} %bitcast.13), channel_id=1, replica_groups=mesh['section'=4,'tok'=8] {'tok'}, use_global_device_ids=true, to_apply=%region_4.5 | all-reduce | flops 6145 | bytes 49160 | tf_op jit(solution)/shard_map/psum | solution.py:94
  143.9 4.2 %fusion.20 = f32[128,6144]{1,0:T(8,128)} fusion(bf16[128,6144]{1,0:T(8,128)(2,1)} %bitcast.40, f32[]{:T(128)} %bitcast.13, f32[6144]{0:T(1024)S(1)} %bitcast.50, f32[128]{0:T(128)S(1)} %slice.18, f32[6144]{0:T(1024)S(1)} %broadcast_divide_fusion, f32[128]{0:T(128)S(1)} %slice.17), kind=kOutput, calls=%fused_computation.32 | convolution fusion | flops 206831616 | bytes 4802048 | tf_op jit(solution)/shard_map/dot_general | solution.py:90
  148.2 129.9 %all-reduce.3.cloned.1.call-done = f32[128,6144]{1,0:T(8,128)} async-done(((f32[128,6144]{1,0:T(8,128)}), f32[128,6144]{1,0:T(8,128)}) %all-reduce.3.cloned.1.call-update) | async-done | bytes 3145744 | tf_op jit(solution)/shard_map/psum | solution.py:96
  278.1 4.4 %divide_bitcast_fusion = f32[1,128,6144]{2,1,0:T(8,128)} fusion(f32[128,6144]{1,0:T(8,128)} %all-reduce.3.cloned.1.call-done, f32[]{:T(128)} %get-tuple-element.240), kind=kLoop, calls=%fused_computation.33 | loop fusion | flops 786432 | bytes 6291460 | tf_op jit(solution)/shard_map/broadcast_in_dim | solution.py:97
  (92 shorter events, 3.0 us)
Async XLA Ops:
  7.2 3.0 %copy-start = (bf16[256,6144]{1,0:T(8,128)(2,1)S(1)}, bf16[256,6144]{1,0:T(8,128)(2,1)}, u32[]{:S(2)}) copy-start(bf16[256,6144]{1,0:T(8,128)(2,1)} %param.14) | copy-start | bytes 9437188
  7.2 270.9 %all-reduce.3.cloned.1.call-start = ((), (), s32[]{:S(2)}) async-start(), calls=%async_computation | async-start | bytes 6291456 | tf_op jit(solution)/shard_map/psum | solution.py:96
  10.1 2.7 copy-start.5
  10.1 2.6 copy-start.6
  19.2 1.6 copy-start.1
  19.2 1.6 copy-start.2
  19.2 1.6 copy-start.3
  22.1 7.1 %collective-permute-start = (bf16[32,6144]{1,0:T(8,128)(2,1)}, bf16[32,6144]{1,0:T(8,128)(2,1)}, u32[]{:S(2)}, u32[]{:S(2)}) collective-permute-start(bf16[32,6144]{1,0:T(8,128)(2,1)} %fusion.32), channel_id=1, source_target_pairs={{0,8},{8,16},{16,24},{1,9},{9,17},{17,25},{2,10},{10,18},{18,26},{... | collective-permute-start | bytes 1179656 | tf_op jit(solution)/shard_map/while/body/eval_jaxpr/ppermute | solution.py:13
  29.2 1.6 copy-start.1
  29.2 1.6 copy-start.2
  29.2 1.6 copy-start.3
  32.1 9.6 %collective-permute-start = (bf16[32,6144]{1,0:T(8,128)(2,1)}, bf16[32,6144]{1,0:T(8,128)(2,1)}, u32[]{:S(2)}, u32[]{:S(2)}) collective-permute-start(bf16[32,6144]{1,0:T(8,128)(2,1)} %fusion.32), channel_id=1, source_target_pairs={{0,8},{8,16},{16,24},{1,9},{9,17},{17,25},{2,10},{10,18},{18,26},{... | collective-permute-start | bytes 1179656 | tf_op jit(solution)/shard_map/while/body/eval_jaxpr/ppermute | solution.py:13
  41.7 1.6 copy-start.1
  41.7 1.6 copy-start.2
  41.7 1.6 copy-start.3
  44.6 9.5 %collective-permute-start = (bf16[32,6144]{1,0:T(8,128)(2,1)}, bf16[32,6144]{1,0:T(8,128)(2,1)}, u32[]{:S(2)}, u32[]{:S(2)}) collective-permute-start(bf16[32,6144]{1,0:T(8,128)(2,1)} %fusion.32), channel_id=1, source_target_pairs={{0,8},{8,16},{16,24},{1,9},{9,17},{17,25},{2,10},{10,18},{18,26},{... | collective-permute-start | bytes 1179656 | tf_op jit(solution)/shard_map/while/body/eval_jaxpr/ppermute | solution.py:13
  54.1 1.6 copy-start.1
  54.1 1.6 copy-start.2
  54.1 1.6 copy-start.3
  57.0 9.5 %collective-permute-start = (bf16[32,6144]{1,0:T(8,128)(2,1)}, bf16[32,6144]{1,0:T(8,128)(2,1)}, u32[]{:S(2)}, u32[]{:S(2)}) collective-permute-start(bf16[32,6144]{1,0:T(8,128)(2,1)} %fusion.32), channel_id=1, source_target_pairs={{0,8},{8,16},{16,24},{1,9},{9,17},{17,25},{2,10},{10,18},{18,26},{... | collective-permute-start | bytes 1179656 | tf_op jit(solution)/shard_map/while/body/eval_jaxpr/ppermute | solution.py:13
  66.5 1.6 copy-start.1
  66.5 1.6 copy-start.2
  66.5 1.6 copy-start.3
  69.4 9.5 %collective-permute-start = (bf16[32,6144]{1,0:T(8,128)(2,1)}, bf16[32,6144]{1,0:T(8,128)(2,1)}, u32[]{:S(2)}, u32[]{:S(2)}) collective-permute-start(bf16[32,6144]{1,0:T(8,128)(2,1)} %fusion.32), channel_id=1, source_target_pairs={{0,8},{8,16},{16,24},{1,9},{9,17},{17,25},{2,10},{10,18},{18,26},{... | collective-permute-start | bytes 1179656 | tf_op jit(solution)/shard_map/while/body/eval_jaxpr/ppermute | solution.py:13
  78.9 1.6 copy-start.1
  78.9 1.6 copy-start.2
  78.9 1.6 copy-start.3
  81.7 9.5 %collective-permute-start = (bf16[32,6144]{1,0:T(8,128)(2,1)}, bf16[32,6144]{1,0:T(8,128)(2,1)}, u32[]{:S(2)}, u32[]{:S(2)}) collective-permute-start(bf16[32,6144]{1,0:T(8,128)(2,1)} %fusion.32), channel_id=1, source_target_pairs={{0,8},{8,16},{16,24},{1,9},{9,17},{17,25},{2,10},{10,18},{18,26},{... | collective-permute-start | bytes 1179656 | tf_op jit(solution)/shard_map/while/body/eval_jaxpr/ppermute | solution.py:13
  91.3 1.6 copy-start.1
  91.3 1.6 copy-start.2
  91.3 1.6 copy-start.3
  94.1 9.5 %collective-permute-start = (bf16[32,6144]{1,0:T(8,128)(2,1)}, bf16[32,6144]{1,0:T(8,128)(2,1)}, u32[]{:S(2)}, u32[]{:S(2)}) collective-permute-start(bf16[32,6144]{1,0:T(8,128)(2,1)} %fusion.32), channel_id=1, source_target_pairs={{0,8},{8,16},{16,24},{1,9},{9,17},{17,25},{2,10},{10,18},{18,26},{... | collective-permute-start | bytes 1179656 | tf_op jit(solution)/shard_map/while/body/eval_jaxpr/ppermute | solution.py:13
  143.9 4.3 %copy-start.4 = (f32[6144]{0:T(1024)}, f32[6144]{0:T(1024)S(1)}, u32[]{:S(2)}) copy-start(f32[6144]{0:T(1024)S(1)} %broadcast_divide_fusion) | copy-start | bytes 73732
Sparse Core Ops, SparseCore 0:
  148.3 129.7 all-reduce.2
where the time goes:
time: 290 us; the launch traced here: 289 us
  waiting for transfers between devices  130 us (45%)
  other arithmetic  45.2 us (16%)
  blocking collectives  37.9 us (13%)
  starting transfers between devices  37.3 us (13%)
  local copies, waits for them, and re-layouts  17.3 us (6%)
  between operations  15.4 us (5%)
  matrix products  5.96 us (2%)
    psum x1, waiting for transfers between devices, body(): lax.psum(about_mean(sum_second, sum_first, own_count, mean_row), 'tok')  130 us
    psum x1, blocking collectives, body(): total_count, channel_sums = lax.psum((own_count, sum_first), 'tok')  37.9 us
    ppermute x7, starting transfers between devices, from_behind(): return lax.ppermute(block, axis, route)  37.3 us
    dynamic_update_slice x7, other arithmetic, tick_step(): stash = lax.dynamic_update_index_in_dim(stash, kept, safe_index, 0)  14.6 us
    dynamic_slice x7, local copies, waits for them, and re-layouts, tick_step(): previous = lax.dynamic_index_in_dim(stash, safe_index, 0, keepdims=False)  12.4 us
    convert_element_type x7, other arithmetic, tick_step(): (current.astype(jnp.float32) + branch_scale[0] * jax.nn.gelu(normed)).ast...  8.82 us
    reduce_sum x7, other arithmetic, layer_norm(): centre = jnp.mean(values, axis=-1, keepdims=True)  8.73 us
  transfers between devices with their start and end apart: 8, of which 1 were waited for; matrix products, arithmetic and copies ran while one was open for 9% of the time, Pallas kernels for 0%

commit v1 on v0

--- a/solution.py
+++ b/solution.py
@@ -93,7 +93,9 @@
     own_count = token_counts.astype(jnp.float32)
     total_count, channel_sums = lax.psum((own_count, sum_first), "tok")
     mean_row = channel_sums / total_count
-    gram_block = lax.psum(about_mean(sum_second, sum_first, own_count, mean_row), "tok")
+    gram_block = jnp.sum(
+        lax.all_gather(about_mean(sum_second, sum_first, own_count, mean_row), "tok"), axis=0
+    )
     return ((gram_block / total_count)[None], mean_row[None])
 
 

time: 290 us -> 653 us (2.25)
  waiting for transfers between devices: 130 us -> 482 us
  other arithmetic: 45.2 us -> 56.3 us
    all_gather x0 -> x1, waiting for transfers between devices: none -> 482 us  [body(): lax.all_gather(about_mean(sum_second, sum_first, own_count, mean_row), 't...]
    psum x1 -> x0, waiting for transfers between devices: 130 us -> none  [body(): lax.psum(about_mean(sum_second, sum_first, own_count, mean_row), 'tok')]
    reduce_sum x0 -> x1, other arithmetic: none -> 11 us  [body(): jnp.sum(lax.all_gather(about_mean(sum_second, sum_first, own_count, mean_...]
  transfers between devices with their start and end apart: 8 -> 8, of which waited for: 1 -> 1; matrix products, arithmetic and copies ran while one was open for 9% -> 4% of each run, Pallas kernels for 0% -> 0%
where the time goes in v1:
time: 653 us; the launch traced here: 652 us
  waiting for transfers between devices  482 us (74%)
  other arithmetic  56.3 us (9%)
  blocking collectives  37.9 us (6%)
  starting transfers between devices  37.3 us (6%)
  local copies, waits for them, and re-layouts  17.3 us (3%)
  between operations  15.4 us (2%)
    all_gather x1, waiting for transfers between devices, body(): lax.all_gather(about_mean(sum_second, sum_first, own_count, mean_row), 't...  482 us
    psum x1, blocking collectives, body(): total_count, channel_sums = lax.psum((own_count, sum_first), 'tok')  37.9 us
    ppermute x7, starting transfers between devices, from_behind(): return lax.ppermute(block, axis, route)  37.3 us
    dynamic_update_slice x7, other arithmetic, tick_step(): stash = lax.dynamic_update_index_in_dim(stash, kept, safe_index, 0)  14.6 us
  transfers between devices with their start and end apart: 8, of which 1 were waited for; matrix products, arithmetic and copies ran while one was open for 4% of the time, Pallas kernels for 0%

profile of v1, /device:TPU:0, one launch (start us, length us, event | category | flops | bytes accessed | tf_op | source)
XLA Modules:
  0.0 652.0 jit_solution(14178271756965897950)
XLA Ops:
  7.2 0.8 compare_and_fusion
  8.0 0.7 compare_select_fusion
  10.2 2.6 gather_fusion
  13.5 3.6 add_convert_fusion
  17.1 0.8 broadcast_in_dim.51
  17.9 1.3 broadcast_in_dim.52
  19.2 84.4 %while.16 = (s32[]{:T(128)}, bf16[32,6144]{1,0:T(8,128)(2,1)}, bf16[4,32,6144]{2,1,0:T(8,128)(2,1)}, pred[]{:T(512)}, s32[]{:T(128)}, /*index=5*/bf16[4,32,6144]...) while((s32[]{:T(128)}, bf16[32,6144]{1,0:T(8,128)(2,1)}, ...), condition=%wide.region_3.4_spmd, body=%wide.region_0.3_spmd.sunk | while | flops 6881320 | bytes 6342548 | solution.py:86
  19.2 1.3 convert_reduce_fusion.2
  20.8 1.3 fusion.32
  22.1 3.3 collective-permute-start
  25.4 1.8 constant_dynamic-slice_fusion.3
  27.1 2.1 bitcast_dynamic-update-slice_fusion.2
  29.2 1.2 convert_reduce_fusion.2
  30.8 1.3 fusion.32
  32.1 5.8 collective-permute-start
  37.9 1.8 constant_dynamic-slice_fusion.3
  39.7 2.1 bitcast_dynamic-update-slice_fusion.2
  41.8 1.2 convert_reduce_fusion.2
  43.3 1.3 fusion.32
  44.6 5.6 collective-permute-start
  50.3 1.8 constant_dynamic-slice_fusion.3
  52.0 2.1 bitcast_dynamic-update-slice_fusion.2
  54.1 1.2 convert_reduce_fusion.2
  55.7 1.3 fusion.32
  57.0 5.7 collective-permute-start
  62.6 1.8 constant_dynamic-slice_fusion.3
  64.4 2.1 bitcast_dynamic-update-slice_fusion.2
  66.5 1.2 convert_reduce_fusion.2
  68.1 1.3 fusion.32
  69.4 5.6 collective-permute-start
  75.0 1.8 constant_dynamic-slice_fusion.3
  76.8 2.1 bitcast_dynamic-update-slice_fusion.2
  78.9 1.2 convert_reduce_fusion.2
  80.5 1.3 fusion.32
  81.7 5.6 collective-permute-start
  87.4 1.8 constant_dynamic-slice_fusion.3
  89.2 2.1 bitcast_dynamic-update-slice_fusion.2
  91.3 1.2 convert_reduce_fusion.2
  92.9 1.3 fusion.32
  94.1 5.6 collective-permute-start
  99.8 1.8 constant_dynamic-slice_fusion.3
  101.5 2.1 bitcast_dynamic-update-slice_fusion.2
  103.6 1.7 fusion.23
  105.3 37.9 %all-reduce = (f32[6144]{0:T(1024)S(1)}, f32[]{:T(128)}) all-reduce(f32[6144]{0:T(1024)S(1)} %bitcast.51, f32[]{:T(128)} %bitcast.13), channel_id=1, replica_groups=mesh['section'=4,'tok'=8] {'tok'}, use_global_device_ids=true, to_apply=%region_4.5 | all-reduce | flops 6145 | bytes 49160 | tf_op jit(solution)/shard_map/psum | solution.py:94
  143.9 4.2 fusion.20
  148.2 481.5 %all-gather.3.cloned.1.call-done = f32[1024,6144]{1,0:T(8,128)} async-done(((f32[128,6144]{1,0:T(8,128)}), f32[1024,6144]{1,0:T(8,128)}) %all-gather.3.cloned.1.call-update) | async-done | bytes 25165840 | tf_op jit(solution)/shard_map/all_gather | solution.py:97
  629.7 11.0 %reduce_sum.37 = f32[128,6144]{1,0:T(8,128)} reduce(f32[8,128,6144]{2,1,0:T(8,128)} %bitcast.40, f32[]{:T(128)} %constant.141.clone.1), dimensions={0}, to_apply=%region_6.7 | reduce | flops 5505024 | bytes 28311556 | tf_op jit(solution)/shard_map/reduce_sum | solution.py:96
  640.7 4.4 divide_bitcast_fusion
  (93 shorter events, 3.7 us)
Async XLA Ops:
  7.2 3.0 copy-start
  7.2 622.5 %all-gather.3.cloned.1.call-start = ((), (), s32[]{:S(2)}) async-start(), calls=%async_computation | async-start | bytes 28311552 | tf_op jit(solution)/shard_map/all_gather | solution.py:97
  10.1 2.7 copy-start.5
  10.1 2.6 copy-start.6
  19.2 1.6 copy-start.1
  19.2 1.6 copy-start.2
  19.2 1.6 copy-start.3
  22.1 7.1 %collective-permute-start = (bf16[32,6144]{1,0:T(8,128)(2,1)}, bf16[32,6144]{1,0:T(8,128)(2,1)}, u32[]{:S(2)}, u32[]{:S(2)}) collective-permute-start(bf16[32,6144]{1,0:T(8,128)(2,1)} %fusion.32), channel_id=1, source_target_pairs={{0,8},{8,16},{16,24},{1,9},{9,17},{17,25},{2,10},{10,18},{18,26},{... | collective-permute-start | bytes 1179656 | tf_op jit(solution)/shard_map/while/body/eval_jaxpr/ppermute | solution.py:13
  29.2 1.6 copy-start.1
  29.2 1.6 copy-start.2
  29.2 1.6 copy-start.3
  32.1 9.6 %collective-permute-start = (bf16[32,6144]{1,0:T(8,128)(2,1)}, bf16[32,6144]{1,0:T(8,128)(2,1)}, u32[]{:S(2)}, u32[]{:S(2)}) collective-permute-start(bf16[32,6144]{1,0:T(8,128)(2,1)} %fusion.32), channel_id=1, source_target_pairs={{0,8},{8,16},{16,24},{1,9},{9,17},{17,25},{2,10},{10,18},{18,26},{... | collective-permute-start | bytes 1179656 | tf_op jit(solution)/shard_map/while/body/eval_jaxpr/ppermute | solution.py:13
  41.7 1.6 copy-start.1
  41.7 1.6 copy-start.2
  41.7 1.6 copy-start.3
  44.6 9.5 %collective-permute-start = (bf16[32,6144]{1,0:T(8,128)(2,1)}, bf16[32,6144]{1,0:T(8,128)(2,1)}, u32[]{:S(2)}, u32[]{:S(2)}) collective-permute-start(bf16[32,6144]{1,0:T(8,128)(2,1)} %fusion.32), channel_id=1, source_target_pairs={{0,8},{8,16},{16,24},{1,9},{9,17},{17,25},{2,10},{10,18},{18,26},{... | collective-permute-start | bytes 1179656 | tf_op jit(solution)/shard_map/while/body/eval_jaxpr/ppermute | solution.py:13
  54.1 1.6 copy-start.1
  54.1 1.6 copy-start.2
  54.1 1.6 copy-start.3
  57.0 9.5 %collective-permute-start = (bf16[32,6144]{1,0:T(8,128)(2,1)}, bf16[32,6144]{1,0:T(8,128)(2,1)}, u32[]{:S(2)}, u32[]{:S(2)}) collective-permute-start(bf16[32,6144]{1,0:T(8,128)(2,1)} %fusion.32), channel_id=1, source_target_pairs={{0,8},{8,16},{16,24},{1,9},{9,17},{17,25},{2,10},{10,18},{18,26},{... | collective-permute-start | bytes 1179656 | tf_op jit(solution)/shard_map/while/body/eval_jaxpr/ppermute | solution.py:13
  66.5 1.6 copy-start.1
  66.5 1.6 copy-start.2
  66.5 1.6 copy-start.3
  69.4 9.5 %collective-permute-start = (bf16[32,6144]{1,0:T(8,128)(2,1)}, bf16[32,6144]{1,0:T(8,128)(2,1)}, u32[]{:S(2)}, u32[]{:S(2)}) collective-permute-start(bf16[32,6144]{1,0:T(8,128)(2,1)} %fusion.32), channel_id=1, source_target_pairs={{0,8},{8,16},{16,24},{1,9},{9,17},{17,25},{2,10},{10,18},{18,26},{... | collective-permute-start | bytes 1179656 | tf_op jit(solution)/shard_map/while/body/eval_jaxpr/ppermute | solution.py:13
  78.9 1.6 copy-start.1
  78.9 1.6 copy-start.2
  78.9 1.6 copy-start.3
  81.7 9.5 %collective-permute-start = (bf16[32,6144]{1,0:T(8,128)(2,1)}, bf16[32,6144]{1,0:T(8,128)(2,1)}, u32[]{:S(2)}, u32[]{:S(2)}) collective-permute-start(bf16[32,6144]{1,0:T(8,128)(2,1)} %fusion.32), channel_id=1, source_target_pairs={{0,8},{8,16},{16,24},{1,9},{9,17},{17,25},{2,10},{10,18},{18,26},{... | collective-permute-start | bytes 1179656 | tf_op jit(solution)/shard_map/while/body/eval_jaxpr/ppermute | solution.py:13
  91.3 1.6 copy-start.1
  91.3 1.6 copy-start.2
  91.3 1.6 copy-start.3
  94.1 9.5 %collective-permute-start = (bf16[32,6144]{1,0:T(8,128)(2,1)}, bf16[32,6144]{1,0:T(8,128)(2,1)}, u32[]{:S(2)}, u32[]{:S(2)}) collective-permute-start(bf16[32,6144]{1,0:T(8,128)(2,1)} %fusion.32), channel_id=1, source_target_pairs={{0,8},{8,16},{16,24},{1,9},{9,17},{17,25},{2,10},{10,18},{18,26},{... | collective-permute-start | bytes 1179656 | tf_op jit(solution)/shard_map/while/body/eval_jaxpr/ppermute | solution.py:13
  143.9 4.3 copy-start.4
Sparse Core Ops, SparseCore 0:
  148.3 481.3 all-gather.2
